TPU v7x, 32 devices: a whole 2x2x4 slice. The times are simulated.
32 devices in a mesh: dp: 2 (over y), ctx: 4 (over z), tp: 4 (over x, core).
Axes of the slice: x: 2, y: 2, z: 4, core: 2. Of those that a mesh axis runs over, the one named last changes fastest.
Arguments:
- layer_input: bfloat16 [2, 4096, 1024], P('dp', 'ctx'), may hold values from -6 to 6
- segments: int32 [2, 4096], P('dp', 'ctx'), may hold values from 0 to 16, as said below
- positions: int32 [2, 4096], P('dp', 'ctx'), may hold values from 0 to 4094, as said below
- w_q: bfloat16 [1024, 1024], P('dp', 'tp'), may hold values from -0.1875 to 0.1875
- w_k: bfloat16 [1024, 1024], P('dp', 'tp'), may hold values from -0.1875 to 0.1875
- w_v: bfloat16 [1024, 1024], P('dp', 'tp'), may hold values from -0.1875 to 0.1875
- w_o: bfloat16 [1024, 1024], P('tp', 'dp'), may hold values from -0.75 to 0.75
- w_in: bfloat16 [1024, 4096], P('dp', 'tp'), may hold values from -0.1875 to 0.1875
- w_out: bfloat16 [4096, 1024], P('tp', 'dp'), may hold values from -0.09375 to 0.09375
- ln1_gain: bfloat16 [1024], P('dp'), may hold values from 0.25 to 1.75
- ln1_bias: bfloat16 [1024], P('dp'), may hold values from -1 to 1
- ln2_gain: bfloat16 [1024], P('dp'), may hold values from 0.25 to 1.75
- ln2_bias: bfloat16 [1024], P('dp'), may hold values from -1 to 1
- cotangent: bfloat16 [2, 4096, 1024], P('dp', 'ctx'), may hold values from -6 to 6
Outputs:
- layer_output: float32 [2, 4096, 1024], P('dp', 'ctx')
- x_grad: float32 [2, 4096, 1024], P('dp', 'ctx')
- w_q_grad: float32 [1024, 1024], P('dp', 'tp')
- w_k_grad: float32 [1024, 1024], P('dp', 'tp')
- w_v_grad: float32 [1024, 1024], P('dp', 'tp')
- w_o_grad: float32 [1024, 1024], P('tp', 'dp')
- w_in_grad: float32 [1024, 4096], P('dp', 'tp')
- w_out_grad: float32 [4096, 1024], P('tp', 'dp')
- ln1_gain_grad: float32 [1024], P('dp')
- ln1_bias_grad: float32 [1024], P('dp')
- ln2_gain_grad: float32 [1024], P('dp')
- ln2_bias_grad: float32 [1024], P('dp')
Inputs may be any that keep to these rules, and one draw needn't show every extreme that they name: `segments`: along a sequence the document number never falls; it is 0 at the first slot and 16 at the last. `positions`: A slot's position is its offset from the first slot of its document.
All inputs are finite; a program needn't handle non-finite values.
Results may differ from a plain program's by a relative error of at most 0.023.
Values may be sent and summed in bfloat16 or wider, within the bound.
No kernel may reach another device: no remote copies, remote signals or barrier semaphores. Data moves between devices by JAX's collectives and lax.ppermute only.
A program may use at most 256 MiB of HBM per device.

v0:
```python
import jax
import jax.numpy as jnp
from jax import lax
from jax.sharding import PartitionSpec as P

D = 1024
H = 16
NEG_BIG = -1e30
SQRT_HALF = 0.7071067811865476
INV_SQRT_TAU = 0.3989422804014327


def rotate_heads(values, positions, head_size, sign):
    half = head_size // 2
    freq = 10000.0 ** (-jnp.arange(half, dtype=jnp.float32) * 2.0 / head_size)
    angles = positions.astype(jnp.float32)[..., None] * freq
    cosine = jnp.cos(angles)[..., None, :]
    sine = sign * jnp.sin(angles)[..., None, :]
    first = values[..., :half]
    second = values[..., half:]
    return jnp.concatenate(
        [first * cosine - second * sine, second * cosine + first * sine], axis=-1
    )


def norm_forward(values, gain, shift):
    centered = values - jnp.mean(values, axis=-1, keepdims=True)
    inverse = lax.rsqrt(jnp.mean(centered * centered, axis=-1, keepdims=True) + 1e-05)
    normed = centered * inverse
    return (normed * gain.astype(jnp.float32) + shift.astype(jnp.float32), normed, inverse)


def norm_backward(incoming, normed, inverse, gain):
    scaled = incoming * gain.astype(jnp.float32)
    inner = (
        scaled
        - jnp.mean(scaled, axis=-1, keepdims=True)
        - normed * jnp.mean(scaled * normed, axis=-1, keepdims=True)
    )
    return (inverse * inner, jnp.sum(incoming * normed, axis=0), jnp.sum(incoming, axis=0))


def body(
    layer_input,
    segments,
    positions,
    w_q,
    w_k,
    w_v,
    w_o,
    w_in,
    w_out,
    ln1_gain,
    ln1_bias,
    ln2_gain,
    ln2_bias,
    cotangent,
):
    seqs, piece_len, width = layer_input.shape
    head_size = D // H
    (
        query_weight,
        key_weight,
        value_weight,
        out_weight,
        in_weight,
        down_weight,
        gain_one,
        shift_one,
        gain_two,
        shift_two,
    ) = (
        lax.all_gather(w_q, "dp", axis=0, tiled=True),
        lax.all_gather(w_k, "dp", axis=0, tiled=True),
        lax.all_gather(w_v, "dp", axis=0, tiled=True),
        lax.all_gather(w_o, "dp", axis=1, tiled=True),
        lax.all_gather(w_in, "dp", axis=0, tiled=True),
        lax.all_gather(w_out, "dp", axis=1, tiled=True),
        lax.all_gather(ln1_gain, "dp", axis=0, tiled=True),
        lax.all_gather(ln1_bias, "dp", axis=0, tiled=True),
        lax.all_gather(ln2_gain, "dp", axis=0, tiled=True),
        lax.all_gather(ln2_bias, "dp", axis=0, tiled=True),
    )
    local_width = query_weight.shape[1]
    heads_here = local_width // head_size
    doc_whole = lax.all_gather(segments, "ctx", axis=1, tiled=True)
    full_len = doc_whole.shape[1]
    row_count = seqs * piece_len
    tokens = layer_input.reshape(row_count, width)
    scale = head_size ** (-0.5)
    doc_low = jnp.min(segments, axis=1)
    doc_high = jnp.max(segments, axis=1)
    share = row_count // lax.axis_size("tp")
    offset = lax.axis_index("tp") * share

    def reduce_heads(partial_sum):
        return lax.psum_scatter(
            partial_sum.astype(jnp.bfloat16), "tp", scatter_dimension=0, tiled=True
        ).astype(jnp.float32)

    def spread_rows(rows_low):
        return lax.all_gather(rows_low, "tp", axis=0, tiled=True)

    def own_rows(whole_rows):
        return lax.dynamic_slice_in_dim(whole_rows, offset, share, 0)

    def project(weight):
        return jnp.dot(tokens, weight, preferred_element_type=jnp.float32).reshape(
            seqs, piece_len, heads_here, head_size
        )

    queries = rotate_heads(project(query_weight), positions, head_size, 1.0).astype(jnp.bfloat16)
    keys = rotate_heads(project(key_weight), positions, head_size, 1.0).astype(jnp.bfloat16)
    values = project(value_weight).astype(jnp.bfloat16)

    def touches():
        meets = (doc_low <= jnp.max(doc_whole, axis=1)) & (jnp.min(doc_whole, axis=1) <= doc_high)
        return (jnp.any(meets), doc_whole)

    def masked_scores(key_piece, doc_keys):
        scores = (
            jnp.einsum("sqhd,skhd->shqk", queries, key_piece, preferred_element_type=jnp.float32)
            * scale
        )
        same = segments[:, None, :, None] == doc_keys[:, None, None, :]
        return jnp.where(same, scores, NEG_BIG)

    start_state = (
        jnp.full((seqs, heads_here, piece_len), NEG_BIG, jnp.float32),
        jnp.zeros((seqs, heads_here, piece_len), jnp.float32),
        jnp.zeros((seqs, piece_len, heads_here, head_size), jnp.float32),
    )
    key_piece = lax.all_gather(keys, "ctx", axis=1, tiled=True)
    value_piece = lax.all_gather(values, "ctx", axis=1, tiled=True)
    needed, doc_keys = touches()

    def forward_update(state):
        run_max, run_total, run_out = state
        scores = masked_scores(key_piece, doc_keys)
        new_max = jnp.maximum(run_max, jnp.max(scores, axis=-1))
        weights_now = jnp.exp(scores - new_max[..., None])
        factor = jnp.exp(run_max - new_max)
        new_total = jnp.sum(weights_now, axis=-1)
        added = jnp.einsum(
            "shqk,skhd->sqhd",
            weights_now.astype(jnp.bfloat16),
            value_piece,
            preferred_element_type=jnp.float32,
        )
        new_out = run_out * jnp.swapaxes(factor, 1, 2)[..., None] + added
        return (new_max, new_total, new_out)

    run_max, run_total, run_out = lax.cond(needed, forward_update, lambda state: state, start_state)
    attended = run_out / jnp.swapaxes(run_total, 1, 2)[..., None]
    log_total = run_max + jnp.log(run_total)
    attended_low = attended.astype(jnp.bfloat16).reshape(row_count, local_width)
    mixed = reduce_heads(jnp.dot(attended_low, out_weight, preferred_element_type=jnp.float32))
    token_rows = own_rows(tokens).astype(jnp.float32)
    hidden_one, normed_one, inverse_one = norm_forward(token_rows + mixed, gain_one, shift_one)
    hidden_low = spread_rows(hidden_one.astype(jnp.bfloat16))
    pre_act = jnp.dot(hidden_low, in_weight, preferred_element_type=jnp.float32)
    activated = jax.nn.gelu(pre_act, approximate=False).astype(jnp.bfloat16)
    branch_two = reduce_heads(jnp.dot(activated, down_weight, preferred_element_type=jnp.float32))
    output, normed_two, inverse_two = norm_forward(hidden_one + branch_two, gain_two, shift_two)
    out_grad = own_rows(cotangent.reshape(row_count, width)).astype(jnp.float32)
    second_grad, gain_two_grad, shift_two_grad = norm_backward(
        out_grad, normed_two, inverse_two, gain_two
    )
    second_low = spread_rows(second_grad.astype(jnp.bfloat16))
    down_grad = jnp.einsum("rf,rd->fd", activated, second_low, preferred_element_type=jnp.float32)
    act_grad = jnp.einsum("rd,fd->rf", second_low, down_weight, preferred_element_type=jnp.float32)
    slope = (
        0.5 * (1.0 + jax.scipy.special.erf(pre_act * SQRT_HALF))
        + pre_act * jnp.exp(-0.5 * pre_act * pre_act) * INV_SQRT_TAU
    )
    pre_grad = (act_grad * slope).astype(jnp.bfloat16)
    in_grad = jnp.einsum("rd,rf->df", hidden_low, pre_grad, preferred_element_type=jnp.float32)
    hidden_grad = second_grad + reduce_heads(
        jnp.einsum("rf,df->rd", pre_grad, in_weight, preferred_element_type=jnp.float32)
    )
    first_grad, gain_one_grad, shift_one_grad = norm_backward(
        hidden_grad, normed_one, inverse_one, gain_one
    )
    first_low = spread_rows(first_grad.astype(jnp.bfloat16))
    out_weight_grad = jnp.einsum(
        "rj,rd->jd", attended_low, first_low, preferred_element_type=jnp.float32
    )
    heads_grad = jnp.einsum("rd,jd->rj", first_low, out_weight, preferred_element_type=jnp.float32)
    heads_grad = heads_grad.astype(jnp.bfloat16).reshape(seqs, piece_len, heads_here, head_size)
    row_dot = jnp.swapaxes(jnp.sum(heads_grad.astype(jnp.float32) * attended, axis=-1), 1, 2)
    back_state = (
        jnp.zeros((seqs, piece_len, heads_here, head_size), jnp.float32),
        jnp.zeros((seqs, full_len, heads_here, head_size), jnp.float32),
        jnp.zeros((seqs, full_len, heads_here, head_size), jnp.float32),
    )
    backward_key_piece = lax.all_gather(keys, "ctx", axis=1, tiled=True)
    backward_value_piece = lax.all_gather(values, "ctx", axis=1, tiled=True)
    needed, backward_doc_keys = touches()

    def backward_update(state):
        scores = masked_scores(backward_key_piece, backward_doc_keys)
        probs = jnp.exp(scores - log_total[..., None])
        value_part = jnp.einsum(
            "shqk,sqhd->skhd",
            probs.astype(jnp.bfloat16),
            heads_grad,
            preferred_element_type=jnp.float32,
        )
        prob_grad = jnp.einsum(
            "sqhd,skhd->shqk", heads_grad, backward_value_piece, preferred_element_type=jnp.float32
        )
        score_grad = (probs * (prob_grad - row_dot[..., None])).astype(jnp.bfloat16)
        query_grad = (
            jnp.einsum(
                "shqk,skhd->sqhd",
                score_grad,
                backward_key_piece,
                preferred_element_type=jnp.float32,
            )
            * scale
        )
        key_part = (
            jnp.einsum("shqk,sqhd->skhd", score_grad, queries, preferred_element_type=jnp.float32)
            * scale
        )
        return (query_grad, key_part, value_part)

    query_grad, key_grad_all, value_grad_all = lax.cond(
        needed, backward_update, lambda state: state, back_state
    )
    key_grad, value_grad = (
        lax.psum_scatter(
            key_grad_all.astype(jnp.bfloat16), "ctx", scatter_dimension=1, tiled=True
        ).astype(jnp.float32),
        lax.psum_scatter(
            value_grad_all.astype(jnp.bfloat16), "ctx", scatter_dimension=1, tiled=True
        ).astype(jnp.float32),
    )
    query_low = (
        rotate_heads(query_grad, positions, head_size, -1.0)
        .astype(jnp.bfloat16)
        .reshape(row_count, local_width)
    )
    key_low = (
        rotate_heads(key_grad, positions, head_size, -1.0)
        .astype(jnp.bfloat16)
        .reshape(row_count, local_width)
    )
    value_low = value_grad.astype(jnp.bfloat16).reshape(row_count, local_width)
    query_weight_grad = jnp.einsum(
        "rd,rj->dj", tokens, query_low, preferred_element_type=jnp.float32
    )
    key_weight_grad = jnp.einsum("rd,rj->dj", tokens, key_low, preferred_element_type=jnp.float32)
    value_weight_grad = jnp.einsum(
        "rd,rj->dj", tokens, value_low, preferred_element_type=jnp.float32
    )
    input_part = jnp.einsum(
        "rj,dj->rd", query_low, query_weight, preferred_element_type=jnp.float32
    )
    input_part = input_part + jnp.einsum(
        "rj,dj->rd", key_low, key_weight, preferred_element_type=jnp.float32
    )
    input_part = input_part + jnp.einsum(
        "rj,dj->rd", value_low, value_weight, preferred_element_type=jnp.float32
    )
    input_grad = first_grad + reduce_heads(input_part)
    norm_terms = jnp.stack([gain_one_grad, shift_one_grad, gain_two_grad, shift_two_grad])[None]
    output, input_grad, norm_terms = (
        lax.all_gather(output.astype(jnp.bfloat16), "tp", axis=0, tiled=True).astype(output.dtype),
        lax.all_gather(input_grad.astype(jnp.bfloat16), "tp", axis=0, tiled=True).astype(
            input_grad.dtype
        ),
        lax.all_gather(norm_terms.astype(jnp.bfloat16), "tp", axis=0, tiled=True).astype(
            norm_terms.dtype
        ),
    )
    norm_terms = jnp.sum(norm_terms, axis=0)
    gain_one_grad, shift_one_grad, gain_two_grad, shift_two_grad = (
        norm_terms[0],
        norm_terms[1],
        norm_terms[2],
        norm_terms[3],
    )
    shares = (
        lax.psum_scatter(
            query_weight_grad.astype(jnp.bfloat16), "dp", scatter_dimension=0, tiled=True
        ).astype(jnp.float32),
        lax.psum_scatter(
            key_weight_grad.astype(jnp.bfloat16), "dp", scatter_dimension=0, tiled=True
        ).astype(jnp.float32),
        lax.psum_scatter(
            value_weight_grad.astype(jnp.bfloat16), "dp", scatter_dimension=0, tiled=True
        ).astype(jnp.float32),
        lax.psum_scatter(
            out_weight_grad.astype(jnp.bfloat16), "dp", scatter_dimension=1, tiled=True
        ).astype(jnp.float32),
        lax.psum_scatter(
            in_grad.astype(jnp.bfloat16), "dp", scatter_dimension=0, tiled=True
        ).astype(jnp.float32),
        lax.psum_scatter(
            down_grad.astype(jnp.bfloat16), "dp", scatter_dimension=1, tiled=True
        ).astype(jnp.float32),
        lax.psum_scatter(
            gain_one_grad.astype(jnp.bfloat16), "dp", scatter_dimension=0, tiled=True
        ).astype(jnp.float32),
        lax.psum_scatter(
            shift_one_grad.astype(jnp.bfloat16), "dp", scatter_dimension=0, tiled=True
        ).astype(jnp.float32),
        lax.psum_scatter(
            gain_two_grad.astype(jnp.bfloat16), "dp", scatter_dimension=0, tiled=True
        ).astype(jnp.float32),
        lax.psum_scatter(
            shift_two_grad.astype(jnp.bfloat16), "dp", scatter_dimension=0, tiled=True
        ).astype(jnp.float32),
    )
    totals = (
        lax.psum(shares[0].astype(jnp.bfloat16), "ctx").astype(jnp.float32),
        lax.psum(shares[1].astype(jnp.bfloat16), "ctx").astype(jnp.float32),
        lax.psum(shares[2].astype(jnp.bfloat16), "ctx").astype(jnp.float32),
        lax.psum(shares[3].astype(jnp.bfloat16), "ctx").astype(jnp.float32),
        lax.psum(shares[4].astype(jnp.bfloat16), "ctx").astype(jnp.float32),
        lax.psum(shares[5].astype(jnp.bfloat16), "ctx").astype(jnp.float32),
        lax.psum(shares[6].astype(jnp.bfloat16), "ctx").astype(jnp.float32),
        lax.psum(shares[7].astype(jnp.bfloat16), "ctx").astype(jnp.float32),
        lax.psum(shares[8].astype(jnp.bfloat16), "ctx").astype(jnp.float32),
        lax.psum(shares[9].astype(jnp.bfloat16), "ctx").astype(jnp.float32),
    )
    return (
        output.reshape(seqs, piece_len, width),
        input_grad.reshape(seqs, piece_len, width),
        totals[0],
        totals[1],
        totals[2],
        totals[3],
        totals[4],
        totals[5],
        totals[6],
        totals[7],
        totals[8],
        totals[9],
    )


def solution(mesh):
    return jax.shard_map(
        body,
        mesh=mesh,
        in_specs=(
            P("dp", "ctx", None),
            P("dp", "ctx"),
            P("dp", "ctx"),
            P("dp", "tp"),
            P("dp", "tp"),
            P("dp", "tp"),
            P("tp", "dp"),
            P("dp", "tp"),
            P("tp", "dp"),
            P("dp"),
            P("dp"),
            P("dp"),
            P("dp"),
            P("dp", "ctx", None),
        ),
        out_specs=(
            P("dp", "ctx", None),
            P("dp", "ctx", None),
            P("dp", "tp"),
            P("dp", "tp"),
            P("dp", "tp"),
            P("tp", "dp"),
            P("dp", "tp"),
            P("tp", "dp"),
            P("dp"),
            P("dp"),
            P("dp"),
            P("dp"),
        ),
        check_vma=False,
    )
```

profile of v0, /device:TPU:0, one launch (start us, length us, event | category | flops | bytes accessed | tf_op | source)
XLA Modules:
  0.0 972.7 jit_solution(8596426434265717203)
XLA Ops:
  8.1 10.4 %all_gather.63 = bf16[1024,256]{1,0:T(8,128)(2,1)S(1)} all-gather(bf16[512,256]{1,0:T(8,128)(2,1)} %param.23), channel_id=1, replica_groups=mesh['dp'=2,'ctx'=4,'tp'=4] {'dp'}, dimensions={0}, use_global_device_ids=true | all-gather | bytes 786432 | tf_op jit(solution)/shard_map/all_gather | solution.py:75
  18.7 3.2 fusion.94
  21.9 8.1 all_gather.61
  30.3 7.3 all_gather.60
  39.0 2.4 fusion.79
  41.4 2.4 fusion.76
  45.1 13.8 %all_gather.59 = s32[1,4096]{1,0:T(1,128)S(1)} all-gather(s32[1,1024]{1,0:T(1,128)S(1)} %copy-done.25), channel_id=1, replica_groups=mesh['dp'=2,'ctx'=4,'tp'=4] {'ctx'}, dimensions={1}, use_global_device_ids=true | all-gather | bytes 20480 | tf_op jit(solution)/shard_map/all_gather | solution.py:86
  62.8 7.0 all_gather.65
  69.8 46.2 %all-gather.15.cloned.1.call-done = bf16[1,4096,4,64]{1,3,2,0:T(8,128)(2,1)} async-done(((bf16[1,1024,4,64]{1,3,2,0:T(8,128)(2,1)}), bf16[1,4096,4,64]{1,3,2,0:T(8,128)(2,1)}) %all-gather.15.cloned.1.call-update) | async-done | bytes 2097168 | tf_op jit(solution)/shard_map/all_gather | solution.py:133
  116.0 81.0 %conditional.2 = (f32[1,4,1024]{2,1,0:T(4,128)S(1)}, f32[1,4,1024]{2,1,0:T(4,128)}, f32[1,1024,4,64]{1,3,2,0:T(8,128)S(1)}, f32[1,4,1024]{2,1,0:T(4,128)S(1)}) conditional(s32[]{:T(128)} %convert_element_type.302, () %tuple.32, (s32[1,1024]{1,0:T(1,128)S(1)}, s32[1,4096]{1,0:T(1,128)S(1)}, bf16[1,1024,4,64]{1,3,2,0:T(8,128)(2,1)S(1)}, ...), branch_computations={%region_4.0_spmd, %region_5.8_spmd} | conditional | flops 4483981312 | bytes 232476736 | solution.py:153
  116.2 4.7 broadcast_compare_fusion
  120.9 25.9 %fusion = (f32[4,1024]{1,0:T(4,128)S(1)}, f32[4,1024,4096]{2,1,0:T(8,128)}) fusion(pred[1024,4096]{1,0:T(8,128)(4,1)} %broadcast_compare_fusion, bf16[1,4096,4,64]{1,3,2,0:T(8,128)(2,1)S(1)} %copy-done.2, bf16[1,1024,4,64]{1,3,2,0:T(8,128)(2,1)S(1)} %get-tuple-element.51), kind=kOutput, calls=%fused_computation.2 | convolution fusion | flops 2197811200 | bytes 73940992 | tf_op jit(solution)/shard_map/cond/branch_1_fun/sqhd,skhd->shqk/dot_general | solution.py:122
  146.8 23.3 %fusion.2 = f32[4,1024]{1,0:T(4,128)} fusion(f32[4,1024,4096]{2,1,0:T(8,128)} %get-tuple-element.155, f32[4,1024]{1,0:T(4,128)S(1)} %broadcast_maximum_fusion, pred[1024,4096]{1,0:T(8,128)(4,1)} %broadcast_compare_fusion), kind=kLoop, calls=%fused_computation.4 | loop fusion | flops 67104768 | bytes 71335936 | tf_op jit(solution)/shard_map/cond/branch_1_fun/reduce_sum | solution.py:143
  170.9 26.1 %fusion.14 = f32[1,1024,4,64]{1,3,2,0:T(8,128)S(1)} fusion(bf16[1,4096,4,64]{1,3,2,0:T(8,128)(2,1)} %get-tuple-element.53, f32[4,1024,4096]{2,1,0:T(8,128)} %get-tuple-element.155, f32[4,1024]{1,0:T(4,128)S(1)} %broadcast_maximum_fusion, pred[1024,4096]{1,0:T(8,128)(4,1)} %broadcast_compare_fusion, f32[1024,4]{0,1:T(4,128)S(1)} %get-tuple-element.144), kind=kOutput, calls=%fused_computation.12 | convolution fusion | flops 2214854656 | bytes 74481664 | tf_op jit(solution)/shard_map/cond/branch_1_fun/shqk,skhd->sqhd/dot_general | solution.py:144
  201.4 4.4 all-gather.1
  205.8 4.4 all-gather.2
  210.2 20.7 %reduce-scatter.13.cloned.1.call-done = bf16[256,1024]{1,0:T(8,128)(2,1)} async-done(((bf16[1024,1024]{1,0:T(8,128)(2,1)}), bf16[256,1024]{1,0:T(8,128)(2,1)}) %reduce-scatter.13.cloned.1.call-update) | async-done | bytes 524304 | tf_op jit(solution)/shard_map/reduce_scatter | solution.py:97
  233.8 2.3 fusion.113
  236.8 22.2 %all-gather.17.cloned.1.call-done = bf16[1024,1024]{1,0:T(8,128)(2,1)} async-done(((bf16[256,1024]{1,0:T(8,128)(2,1)}), bf16[1024,1024]{1,0:T(8,128)(2,1)}) %all-gather.17.cloned.1.call-update) | async-done | bytes 2097168 | tf_op jit(solution)/shard_map/all_gather | solution.py:102
  259.1 14.3 %fusion.50 = (bf16[1024,1024]{1,0:T(8,128)(2,1)}, f32[1024,1024]{1,0:T(8,128)}) fusion(bf16[1024,1024]{1,0:T(8,128)(2,1)} %all-gather.17.cloned.1.call-done, bf16[1024,1024]{1,0:T(8,128)(2,1)} %all-gather.19.cloned.1.call-done), kind=kOutput, calls=%fused_computation.46 | convolution fusion | flops 2215641088 | bytes 10485760 | tf_op jit(solution)/shard_map/dot_general | solution.py:161
  273.4 20.1 %all-gather.21.cloned.1.call-done = bf16[1024,1024]{1,0:T(8,128)(2,1)} async-done(((bf16[1024,512]{1,0:T(8,128)(2,1)}), bf16[1024,1024]{1,0:T(8,128)(2,1)}) %all-gather.21.cloned.1.call-update) | async-done | bytes 2097168 | tf_op jit(solution)/shard_map/all_gather | solution.py:78
  293.5 5.9 convolution_convert_fusion.3
  299.5 4.4 all-gather.3
  303.9 4.4 all-gather.4
  308.3 22.5 %reduce-scatter.15.cloned.1.call-done = bf16[256,1024]{1,0:T(8,128)(2,1)} async-done(((bf16[1024,1024]{1,0:T(8,128)(2,1)}), bf16[256,1024]{1,0:T(8,128)(2,1)}) %reduce-scatter.15.cloned.1.call-update) | async-done | bytes 524304 | tf_op jit(solution)/shard_map/reduce_scatter | solution.py:97
  332.7 2.1 fusion.109
  334.8 2.5 fusion.120
  337.5 22.5 %all-gather.25.cloned.1.call-done = bf16[1024,1024]{1,0:T(8,128)(2,1)} async-done(((bf16[256,1024]{1,0:T(8,128)(2,1)}), bf16[1024,1024]{1,0:T(8,128)(2,1)}) %all-gather.25.cloned.1.call-update) | async-done | bytes 2097168 | tf_op jit(solution)/shard_map/all_gather | solution.py:102
  360.0 6.3 fusion.56
  367.7 3.7 convolution_convert_fusion.2
  371.5 31.3 %reduce-scatter.17.cloned.1.call-done = bf16[256,1024]{1,0:T(8,128)(2,1)} async-done(((bf16[1024,1024]{1,0:T(8,128)(2,1)}), bf16[256,1024]{1,0:T(8,128)(2,1)}) %reduce-scatter.17.cloned.1.call-update) | async-done | bytes 524304 | tf_op jit(solution)/shard_map/reduce_scatter | solution.py:97
  402.8 2.4 multiply_reduce_fusion
  405.2 2.8 fusion.119
  408.0 22.7 %all-gather.27.cloned.1.call-done = bf16[1024,1024]{1,0:T(8,128)(2,1)} async-done(((bf16[256,1024]{1,0:T(8,128)(2,1)}), bf16[1024,1024]{1,0:T(8,128)(2,1)}) %all-gather.27.cloned.1.call-update) | async-done | bytes 2097168 | tf_op jit(solution)/shard_map/all_gather | solution.py:102
  430.7 2.6 convolution_convert_fusion.6
  434.2 129.8 %conditional.3 = (bf16[1,4096,4,64]{1,3,2,0:T(8,128)(2,1)}, bf16[1,4096,4,64]{1,3,2,0:T(8,128)(2,1)}, f32[1,1024,4,32]{1,3,2,0:T(8,128)}, f32[1,1024,4,32]{1,3,2,0:T(8,128)S(1)}) conditional(s32[]{:T(128)} %convert_element_type.302, () %tuple.34, (s32[1,1024]{1,0:T(1,128)S(1)}, s32[1,4096]{1,0:T(1,128)S(1)}, ...), branch_computations={%region_20.21_spmd, %region_21.22_spmd} | conditional | flops 10911748096 | bytes 349294720 | solution.py:228
  434.3 4.7 broadcast_compare_fusion.1
  439.0 23.1 %fusion.34 = f32[4,1024,4096]{2,1,0:T(8,128)} fusion(bf16[1,4096,4,64]{1,3,2,0:T(8,128)(2,1)S(1)} %get-tuple-element.57, bf16[1,1024,4,64]{1,3,2,0:T(8,128)(2,1)S(1)} %get-tuple-element.56), kind=kOutput, calls=%fused_computation.31 | convolution fusion | flops 2147483648 | bytes 69730304 | tf_op jit(solution)/shard_map/cond/branch_1_fun/sqhd,skhd->shqk/dot_general | solution.py:122
  462.2 28.2 %fusion.28 = bf16[1,4096,4,64]{1,3,2,0:T(8,128)(2,1)} fusion(f32[4,1024,4096]{2,1,0:T(8,128)} %fusion.34, f32[4,1024]{1,0:T(4,128)S(1)} %add_bitcast_fusion, pred[1024,4096]{1,0:T(8,128)(4,1)} %broadcast_compare_fusion.1, bf16[1,1024,4,64]{1,3,2,0:T(8,128)(2,1)S(1)} %get-tuple-element.60), kind=kOutput, calls=%fused_computation.27 | convolution fusion | flops 2214592512 | bytes 73940992 | tf_op jit(solution)/shard_map/cond/branch_1_fun/shqk,sqhd->skhd/dot_general | solution.py:203
  490.3 41.9 %multiply_convert_fusion = bf16[4,1024,4096]{2,1,0:T(8,128)(2,1)} fusion(f32[4,1024,4096]{2,1,0:T(8,128)} %fusion.34, f32[4,1024]{1,0:T(4,128)S(1)} %bitcast.238, f32[4,1024]{1,0:T(4,128)S(1)} %add_bitcast_fusion, pred[1024,4096]{1,0:T(8,128)(4,1)} %broadcast_compare_fusion.1, bf16[1,4096,4,64]{1,3,2,0:T(8,128)(2,1)} %get-tuple-element.61, ...), kind=kOutput, calls=%fused_computation.19 | convolution fusion | flops 2248146944 | bytes 107511808 | tf_op jit(solution)/shard_map/cond/branch_1_fun/sqhd,skhd->shqk/dot_general | solution.py:209
  532.2 15.6 %fusion.39 = f32[1,1024,4,64]{1,3,2,0:T(8,128)S(1)} fusion(bf16[4,1024,4096]{2,1,0:T(8,128)(2,1)} %multiply_convert_fusion, bf16[1,4096,4,64]{1,3,2,0:T(8,128)(2,1)S(1)} %copy-done.4), kind=kOutput, calls=%fused_computation.34 | convolution fusion | flops 2147745792 | bytes 36700160 | tf_op jit(solution)/shard_map/cond/branch_1_fun/shqk,skhd->sqhd/dot_general | solution.py:214
  547.8 15.1 %fusion.27 = bf16[1,4096,4,64]{1,3,2,0:T(8,128)(2,1)} fusion(bf16[4,1024,4096]{2,1,0:T(8,128)(2,1)} %multiply_convert_fusion, bf16[1,1024,4,64]{1,3,2,0:T(8,128)(2,1)S(1)} %get-tuple-element.56), kind=kOutput, calls=%fused_computation.26 | convolution fusion | flops 2149580800 | bytes 36175872 | tf_op jit(solution)/shard_map/cond/branch_1_fun/shqk,sqhd->skhd/dot_general | solution.py:223
  565.6 5.3 convolution_convert_fusion.1
  571.0 6.0 convolution_convert_fusion
  577.1 3.2 convolution_convert_fusion.5
  580.4 27.4 %reduce-scatter.21.cloned.1.call-done = bf16[1,1024,4,64]{1,3,2,0:T(8,128)(2,1)} async-done(((bf16[1,4096,4,64]{1,3,2,0:T(8,128)(2,1)}), bf16[1,1024,4,64]{1,3,2,0:T(8,128)(2,1)}) %reduce-scatter.21.cloned.1.call-update) | async-done | bytes 524304 | tf_op jit(solution)/shard_map/reduce_scatter | solution.py:235
  607.8 2.5 fusion.100
  610.4 43.1 %reduce-scatter.19.cloned.1.call-done = bf16[1,1024,4,64]{1,3,2,0:T(8,128)(2,1)} async-done(((bf16[1,4096,4,64]{1,3,2,0:T(8,128)(2,1)}), bf16[1,1024,4,64]{1,3,2,0:T(8,128)(2,1)}) %reduce-scatter.19.cloned.1.call-update) | async-done | bytes 524304 | tf_op jit(solution)/shard_map/reduce_scatter | solution.py:232
  656.2 3.2 fusion.97
  659.4 3.2 fusion.103
  667.2 20.3 %reduce-scatter.33.cloned.1.call-done = bf16[512,1024]{1,0:T(8,128)(2,1)} async-done(((bf16[1024,1024]{1,0:T(8,128)(2,1)}), bf16[512,1024]{1,0:T(8,128)(2,1)}) %reduce-scatter.33.cloned.1.call-update) | async-done | bytes 1048592 | tf_op jit(solution)/shard_map/reduce_scatter | solution.py:297
  687.5 34.2 %reduce-scatter.35.cloned.1.call-done = bf16[1024,512]{1,0:T(8,128)(2,1)} async-done(((bf16[1024,1024]{1,0:T(8,128)(2,1)}), bf16[1024,512]{1,0:T(8,128)(2,1)}) %reduce-scatter.35.cloned.1.call-update) | async-done | bytes 1048592 | tf_op jit(solution)/shard_map/reduce_scatter | solution.py:300
  721.7 16.8 %reduce-scatter.31.cloned.1.call-done = bf16[256,512]{1,0:T(8,128)(2,1)} async-done(((bf16[256,1024]{1,0:T(8,128)(2,1)}), bf16[256,512]{1,0:T(8,128)(2,1)}) %reduce-scatter.31.cloned.1.call-update) | async-done | bytes 262160 | tf_op jit(solution)/shard_map/reduce_scatter | solution.py:294
  738.5 17.5 %reduce-scatter.29.cloned.1.call-done = bf16[512,256]{0,1:T(8,128)(2,1)} async-done(((bf16[1024,256]{0,1:T(8,128)(2,1)}), bf16[512,256]{0,1:T(8,128)(2,1)}) %reduce-scatter.29.cloned.1.call-update) | async-done | bytes 262160 | tf_op jit(solution)/shard_map/reduce_scatter | solution.py:291
  756.0 17.3 %reduce-scatter.27.cloned.1.call-done = bf16[512,256]{0,1:T(8,128)(2,1)} async-done(((bf16[1024,256]{0,1:T(8,128)(2,1)}), bf16[512,256]{0,1:T(8,128)(2,1)}) %reduce-scatter.27.cloned.1.call-update) | async-done | bytes 262160 | tf_op jit(solution)/shard_map/reduce_scatter | solution.py:288
  773.3 17.5 %reduce-scatter.25.cloned.1.call-done = bf16[512,256]{0,1:T(8,128)(2,1)} async-done(((bf16[1024,256]{0,1:T(8,128)(2,1)}), bf16[512,256]{0,1:T(8,128)(2,1)}) %reduce-scatter.25.cloned.1.call-update) | async-done | bytes 262160 | tf_op jit(solution)/shard_map/reduce_scatter | solution.py:285
  790.9 34.1 %reduce-scatter.23.cloned.1.call-done = bf16[256,1024]{1,0:T(8,128)(2,1)} async-done(((bf16[1024,1024]{1,0:T(8,128)(2,1)}), bf16[256,1024]{1,0:T(8,128)(2,1)}) %reduce-scatter.23.cloned.1.call-update) | async-done | bytes 524304 | tf_op jit(solution)/shard_map/reduce_scatter | solution.py:97
  829.5 4.4 bitcast_convert_fusion.1
  833.9 5.3 all_gather.77
  839.3 5.0 all-reduce.6
  844.6 12.0 %all-reduce.4 = (bf16[512]{0:T(512)(128)(2,1)S(1)}, bf16[512]{0:T(512)(128)(2,1)S(1)}, bf16[512]{0:T(512)(128)(2,1)S(1)}, bf16[512]{0:T(512)(128)(2,1)S(1)}) all-reduce(bf16[512]{0:T(512)(128)(2,1)S(1)} %dynamic-slice.3, bf16[512]{0:T(512)(128)(2,1)S(1)} %dynamic-slice.5, ...), channel_id=1, replica_groups=mesh['dp'=2,'ctx'=4,'tp'=4] {'ctx'}, use_global_device_ids=true, to_apply=%region_43.44 | all-reduce | flops 2048 | bytes 8192 | tf_op jit(solution)/shard_map/psum | solution.py:323
  859.0 90.2 %all-reduce.9.cloned.1.call-done = (bf16[512,256]{0,1:T(8,128)(2,1)}, bf16[512,256]{0,1:T(8,128)(2,1)}, bf16[512,256]{0,1:T(8,128)(2,1)}, bf16[256,512]{1,0:T(8,...) async-done(((bf16[512,256]{0,1:T(8,128)(2,1)}, bf16[512,256]{0,1:T(8,128)(2,1)}, bf16[512,256]{0,1:T(8,128)(2,1)}, bf16[256,512]{1,0:T(8,128)(2,1)}, ...) | async-done | bytes 3145744 | tf_op jit(solution)/shard_map/psum | solution.py:317
  956.7 2.8 convert_element_type.349
  961.1 4.1 bitcast_convert_fusion
  (192 shorter events, 43.4 us)
Async XLA Ops:
  8.0 13.9 %copy-start.29 = (s32[1,1024]{1,0:T(1,128)S(1)}, s32[1,1024]{1,0:T(1,128)}, u32[]{:S(2)}) copy-start(s32[1,1024]{1,0:T(1,128)} %param.20) | copy-start | bytes 12292
  8.0 13.9 %copy-start.22 = (bf16[512,256]{1,0:T(8,128)(2,1)S(1)}, bf16[512,256]{1,0:T(8,128)(2,1)}, u32[]{:S(2)}) copy-start(bf16[512,256]{1,0:T(8,128)(2,1)} %param.22) | copy-start | bytes 786436
  8.0 61.8 %all-gather.31.cloned.1.call-start = ((), (), s32[]{:S(2)}) async-start(), calls=%async_computation.32 | async-start | bytes 2621440 | tf_op jit(solution)/shard_map/all_gather | solution.py:134
  18.4 11.9 %copy-start.5 = (bf16[1024,256]{1,0:T(8,128)(2,1)}, bf16[1024,256]{1,0:T(8,128)(2,1)S(1)}, u32[]{:S(2)}) copy-start(bf16[1024,256]{1,0:T(8,128)(2,1)S(1)} %all_gather.63) | copy-start | bytes 1572868
  18.4 11.9 %copy-start.23 = (bf16[512,256]{1,0:T(8,128)(2,1)S(1)}, bf16[512,256]{1,0:T(8,128)(2,1)}, u32[]{:S(2)}) copy-start(bf16[512,256]{1,0:T(8,128)(2,1)} %param.21) | copy-start | bytes 786436
  21.9 94.1 %all-gather.15.cloned.1.call-start = ((), (), s32[]{:S(2)}) async-start(), calls=%async_computation.12 | async-start | bytes 2621440 | tf_op jit(solution)/shard_map/all_gather | solution.py:133
  30.1 13.7 %copy-start.7 = (bf16[1024,256]{1,0:T(8,128)(2,1)}, bf16[1024,256]{1,0:T(8,128)(2,1)S(1)}, u32[]{:S(2)}) copy-start(bf16[1024,256]{1,0:T(8,128)(2,1)S(1)} %all_gather.61) | copy-start | bytes 1572868
  37.6 6.2 copy-start.9
  39.0 4.8 copy-start.16
  41.4 3.7 copy-start.25
  43.8 19.0 %copy-start.24 = (bf16[256,512]{1,0:T(8,128)(2,1)S(1)}, bf16[256,512]{1,0:T(8,128)(2,1)}, u32[]{:S(2)}) copy-start(bf16[256,512]{1,0:T(8,128)(2,1)} %param.24) | copy-start | bytes 786436
  45.0 185.9 %reduce-scatter.13.cloned.1.call-start = ((), (), s32[]{:S(2)}) async-start(), calls=%async_computation.13 | async-start | bytes 2621440 | tf_op jit(solution)/shard_map/reduce_scatter | solution.py:97
  69.8 128.1 %copy-start.15 = (bf16[256,1024]{1,0:T(8,128)(2,1)}, bf16[256,1024]{1,0:T(8,128)(2,1)S(1)}, u32[]{:S(2)}) copy-start(bf16[256,1024]{1,0:T(8,128)(2,1)S(1)} %all_gather.65) | copy-start | bytes 1572868
  116.2 4.8 copy-start.2
  197.0 4.4 copy-start.30
  197.0 8.8 copy-start.31
  197.9 0.8 copy-start.13
  200.8 36.0 %all-gather.19.cloned.1.call-start = ((), (), s32[]{:S(2)}) async-start(), calls=%async_computation.15 | async-start | bytes 3145728 | tf_op jit(solution)/shard_map/all_gather | solution.py:77
  201.4 57.7 %all-gather.17.cloned.1.call-start = ((), (), s32[]{:S(2)}) async-start(), calls=%async_computation.14 | async-start | bytes 2621440 | tf_op jit(solution)/shard_map/all_gather | solution.py:102
  236.1 57.3 %all-gather.21.cloned.1.call-start = ((), (), s32[]{:S(2)}) async-start(), calls=%async_computation.16 | async-start | bytes 3145728 | tf_op jit(solution)/shard_map/all_gather | solution.py:78
  236.7 94.0 %reduce-scatter.15.cloned.1.call-start = ((), (), s32[]{:S(2)}) async-start(), calls=%async_computation.17 | async-start | bytes 2621440 | tf_op jit(solution)/shard_map/reduce_scatter | solution.py:97
  293.5 6.0 copy-start.32
  293.5 10.4 %copy-start.33 = (bf16[512]{0:T(512)(128)(2,1)S(1)}, bf16[512]{0:T(512)(128)(2,1)}, u32[]{:S(2)}) copy-start(bf16[512]{0:T(512)(128)(2,1)} %param.30) | copy-start | bytes 3076
  293.5 37.3 %copy-start = (bf16[256,1024]{1,0:T(8,128)(2,1)S(1)}, bf16[256,1024]{1,0:T(8,128)(2,1)}, u32[]{:S(2)}) copy-start(bf16[256,1024]{1,0:T(8,128)(2,1)} %reduce-scatter.13.cloned.1.call-done) | copy-start | bytes 1572868
  299.4 60.6 %all-gather.25.cloned.1.call-start = ((), (), s32[]{:S(2)}) async-start(), calls=%async_computation.19 | async-start | bytes 2621440 | tf_op jit(solution)/shard_map/all_gather | solution.py:102
  337.3 65.5 %reduce-scatter.17.cloned.1.call-start = ((), (), s32[]{:S(2)}) async-start(), calls=%async_computation.20 | async-start | bytes 2621440 | tf_op jit(solution)/shard_map/reduce_scatter | solution.py:97
  360.0 7.7 copy-start.35
  366.4 1.3 copy-start.37
  371.5 59.3 %all-gather.27.cloned.1.call-start = ((), (), s32[]{:S(2)}) async-start(), calls=%async_computation.21 | async-start | bytes 2621440 | tf_op jit(solution)/shard_map/all_gather | solution.py:102
  408.0 199.8 %reduce-scatter.21.cloned.1.call-start = ((), (), s32[]{:S(2)}) async-start(), calls=%async_computation.23 | async-start | bytes 2621440 | tf_op jit(solution)/shard_map/reduce_scatter | solution.py:235
  430.7 3.5 copy-start.1
  434.2 4.8 copy-start.3
  434.3 27.9 %copy-start.20 = (bf16[1,1024,4,64]{1,3,2,0:T(8,128)(2,1)}, bf16[1,1024,4,64]{1,3,2,0:T(8,128)(2,1)S(1)}, u32[]{:S(2)}) copy-start(bf16[1,1024,4,64]{1,3,2,0:T(8,128)(2,1)S(1)} %get-tuple-element.60) | copy-start | bytes 1572868 | tf_op jit(solution)/shard_map/cond
  490.3 41.9 %copy-start.4 = (bf16[1,4096,4,64]{1,3,2,0:T(8,128)(2,1)S(1)}, bf16[1,4096,4,64]{1,3,2,0:T(8,128)(2,1)}, u32[]{:S(2)}) copy-start(bf16[1,4096,4,64]{1,3,2,0:T(8,128)(2,1)} %copy-done.3) | copy-start | bytes 6291460 | tf_op jit(solution)/shard_map/cond
  564.0 1.6 copy-start.34
  564.0 89.5 %reduce-scatter.19.cloned.1.call-start = ((), (), s32[]{:S(2)}) async-start(), calls=%async_computation.22 | async-start | bytes 2621440 | tf_op jit(solution)/shard_map/reduce_scatter | solution.py:232
  564.8 122.7 %reduce-scatter.33.cloned.1.call-start = ((), (), s32[]{:S(2)}) async-start(), calls=%async_computation.30 | async-start | bytes 3145728 | tf_op jit(solution)/shard_map/reduce_scatter | solution.py:297
  570.9 6.1 copy-start.14
  570.9 150.8 %reduce-scatter.35.cloned.1.call-start = ((), (), s32[]{:S(2)}) async-start(), calls=%async_computation.31 | async-start | bytes 3145728 | tf_op jit(solution)/shard_map/reduce_scatter | solution.py:300
  577.0 30.9 %copy-start.11 = (bf16[1,1024,1024]{2,1,0:T(8,128)(2,1)S(1)}, bf16[1,1024,1024]{2,1,0:T(8,128)(2,1)}, u32[]{:S(2)}) copy-start(bf16[1,1024,1024]{2,1,0:T(8,128)(2,1)} %param.18) | copy-start | bytes 6291460
  577.0 77.7 %copy-start.17 = (f32[1024,32]{0,1:T(8,128)S(1)}, f32[1024,32]{0,1:T(8,128)}, u32[]{:S(2)}) copy-start(f32[1024,32]{0,1:T(8,128)} %copy-done.16) | copy-start | bytes 393220
  577.0 77.7 %copy-start.21 = (f32[1024,32]{0,1:T(8,128)S(1)}, f32[1024,32]{0,1:T(8,128)}, u32[]{:S(2)}) copy-start(f32[1024,32]{0,1:T(8,128)} %get-tuple-element.169) | copy-start | bytes 393220
  577.0 161.5 %reduce-scatter.31.cloned.1.call-start = ((), (), s32[]{:S(2)}) async-start(), calls=%async_computation.29 | async-start | bytes 786432 | tf_op jit(solution)/shard_map/reduce_scatter | solution.py:294
  580.3 175.6 %reduce-scatter.29.cloned.1.call-start = ((), (), s32[]{:S(2)}) async-start(), calls=%async_computation.28 | async-start | bytes 786432 | tf_op jit(solution)/shard_map/reduce_scatter | solution.py:291
  610.4 162.9 %reduce-scatter.27.cloned.1.call-start = ((), (), s32[]{:S(2)}) async-start(), calls=%async_computation.27 | async-start | bytes 786432 | tf_op jit(solution)/shard_map/reduce_scatter | solution.py:288
  656.2 6.5 copy-start.10
  659.3 131.5 %reduce-scatter.25.cloned.1.call-start = ((), (), s32[]{:S(2)}) async-start(), calls=%async_computation.26 | async-start | bytes 786432 | tf_op jit(solution)/shard_map/reduce_scatter | solution.py:285
  659.4 4.0 copy-start.8
  662.6 1.6 copy-start.6
  662.6 1.6 copy-start.19
  662.6 162.3 %reduce-scatter.23.cloned.1.call-start = ((), (), s32[]{:S(2)}) async-start(), calls=%async_computation.24 | async-start | bytes 2621440 | tf_op jit(solution)/shard_map/reduce_scatter | solution.py:97
  666.4 158.6 %copy-start.12 = (f32[256,1024]{1,0:T(8,128)S(1)}, f32[256,1024]{1,0:T(8,128)}, u32[]{:S(2)}) copy-start(f32[256,1024]{1,0:T(8,128)} %get-tuple-element.147) | copy-start | bytes 3145732
  666.4 161.8 %copy-start.36 = (u32[32]{0:T(128)S(1)}, u32[32]{0:T(128)}, u32[]{:S(2)}) copy-start(u32[32]{0:T(128)} %constant.140) | copy-start | bytes 388
  666.4 163.0 %copy-start.26 = (bf16[1024]{0:T(1024)(128)(2,1)S(1)}, bf16[1024]{0:T(1024)(128)(2,1)}, u32[]{:S(2)}) copy-start(bf16[1024]{0:T(1024)(128)(2,1)} %get-tuple-element.117) | copy-start | bytes 6148
  666.4 163.1 %all-gather.23.cloned.1.call-start = ((), (), s32[]{:S(2)}) async-start(), calls=%async_computation.18 | async-start | bytes 2621440 | tf_op jit(solution)/shard_map/all_gather | solution.py:269
  667.1 282.0 %all-reduce.9.cloned.1.call-start = ((), (), s32[]{:S(2)}) async-start(), calls=%async_computation.33 | async-start | bytes 6291456 | tf_op jit(solution)/shard_map/psum | solution.py:317
  790.8 170.3 %all-gather.29.cloned.1.call-start = ((), (), s32[]{:S(2)}) async-start(), calls=%async_computation.25 | async-start | bytes 2621440 | tf_op jit(solution)/shard_map/all_gather | solution.py:270
  827.0 6.9 copy-start.28
  827.0 6.9 copy-start.27
  949.1 10.3 %copy-start.18 = (bf16[1024,512]{1,0:T(8,128)(2,1)S(1)}, bf16[1024,512]{1,0:T(8,128)(2,1)}, u32[]{:S(2)}) copy-start(bf16[1024,512]{1,0:T(8,128)(2,1)} %get-tuple-element.139) | copy-start | bytes 3145732
Sparse Core Ops, SparseCore 0:
  22.0 47.3 all-gather.30
  71.5 44.4 all-gather.14
  200.9 29.9 reduce-scatter.12
  337.4 22.5 all-gather.24
  408.1 22.5 all-gather.26
  564.1 43.6 reduce-scatter.20
  610.7 42.8 reduce-scatter.18
  656.4 31.0 reduce-scatter.32
  689.8 31.8 reduce-scatter.34
  723.8 14.6 reduce-scatter.30
  741.3 14.6 reduce-scatter.28
  758.6 14.6 reduce-scatter.26
  776.1 14.6 reduce-scatter.24
  793.8 31.1 reduce-scatter.22
  827.7 121.4 all-reduce.8
Sparse Core Ops, SparseCore 1:
  202.8 31.7 all-gather.18
  236.6 22.4 all-gather.16
  260.5 32.9 all-gather.20
  299.5 31.2 reduce-scatter.14
  371.5 31.2 reduce-scatter.16
  669.3 21.6 all-gather.22
  827.1 22.5 all-gather.28
where the time goes:
time: 978 us; the launch traced here: 973 us
  waiting for transfers between devices  529 us (54%)
  matrix products  246 us (25%)
  blocking collectives  86.4 us (9%)
  other arithmetic  78 us (8%)
  between operations  19.7 us (2%)
  local copies, waits for them, and re-layouts  12 us (1%)
    reduce_scatter x4, waiting for transfers between devices, reduce_heads(): lax.psum_scatter(partial_sum.astype(jnp.bfloat16), 'tp', scatter_dimensio...  109 us
    psum x1, waiting for transfers between devices, body(): lax.psum(shares[0].astype(jnp.bfloat16), 'ctx').astype(jnp.float32)  90.2 us
    all_gather x3, waiting for transfers between devices, spread_rows(): return lax.all_gather(rows_low, 'tp', axis=0, tiled=True)  67.4 us
    dot_general x2, matrix products, masked_scores(): jnp.einsum('sqhd,skhd->shqk', queries, key_piece, preferred_element_type=...  49 us
    all_gather x1, waiting for transfers between devices, body(): key_piece = lax.all_gather(keys, 'ctx', axis=1, tiled=True)  46.2 us
    reduce_scatter x1, waiting for transfers between devices, body(): lax.psum_scatter(key_grad_all.astype(jnp.bfloat16), 'ctx', scatter_dimens...  43.1 us
    dot_general x1, matrix products, backward_update(): jnp.einsum('sqhd,skhd->shqk', heads_grad, backward_value_piece, preferred...  41.9 us
    reduce_scatter x1, waiting for transfers between devices, body(): lax.psum_scatter(down_grad.astype(jnp.bfloat16), 'dp', scatter_dimension=...  34.2 us
  transfers between devices with their start and end apart: 22, of which 18 were waited for; matrix products, arithmetic and copies ran while one was open for 8% of the time, Pallas kernels for 0%

commit v1 on v0

--- a/solution.py
+++ b/solution.py
@@ -2,6 +2,7 @@
 import jax.numpy as jnp
 from jax import lax
 from jax.sharding import PartitionSpec as P
+from jax.lax import all_gather
 
 D = 1024
 H = 16
@@ -56,6 +57,14 @@
     ln2_bias,
     cotangent,
 ):
+
+    def cut_stops_all(panel, load):
+        return jnp.split(
+            all_gather(jnp.concatenate([panel, load], 0), "ctx", axis=1, tiled=True),
+            [panel.shape[0]],
+            axis=0,
+        )
+
     seqs, piece_len, width = layer_input.shape
     head_size = D // H
     (
@@ -130,8 +139,7 @@
         jnp.zeros((seqs, heads_here, piece_len), jnp.float32),
         jnp.zeros((seqs, piece_len, heads_here, head_size), jnp.float32),
     )
-    key_piece = lax.all_gather(keys, "ctx", axis=1, tiled=True)
-    value_piece = lax.all_gather(values, "ctx", axis=1, tiled=True)
+    key_piece, value_piece = cut_stops_all(keys, values)
     needed, doc_keys = touches()
 
     def forward_update(state):

time: 978 us -> 1080 us (1.10)
  waiting for transfers between devices: 529 us -> 626 us
    all_gather x2 -> x3, waiting for transfers between devices: 46.2 us -> 147 us  [the longest x1 57.5 us: cut_stops_all(): all_gather(jnp.concatenate([panel, load], 0), 'ctx', axis=1, tiled=True)]
  transfers between devices with their start and end apart: 22 -> 23, of which waited for: 18 -> 20; matrix products, arithmetic and copies ran while one was open for 8% -> 7% of each run, Pallas kernels for 0% -> 0%
where the time goes in v1:
time: 1080 us
  waiting for transfers between devices  626 us (58%)
  matrix products  246 us (23%)
  blocking collectives  86.1 us (8%)
  other arithmetic  82.5 us (8%)
  between operations  19.7 us (2%)
  local copies, waits for them, and re-layouts  13.7 us (1%)
    reduce_scatter x4, waiting for transfers between devices, reduce_heads(): lax.psum_scatter(partial_sum.astype(jnp.bfloat16), 'tp', scatter_dimensio...  108 us
    psum x1, waiting for transfers between devices, body(): lax.psum(shares[0].astype(jnp.bfloat16), 'ctx').astype(jnp.float32)  90.2 us
    all_gather x3, waiting for transfers between devices, spread_rows(): return lax.all_gather(rows_low, 'tp', axis=0, tiled=True)  64.6 us
    all_gather x1, waiting for transfers between devices, cut_stops_all(): all_gather(jnp.concatenate([panel, load], 0), 'ctx', axis=1, tiled=True)  57.5 us
    dot_general x2, matrix products, masked_scores(): jnp.einsum('sqhd,skhd->shqk', queries, key_piece, preferred_element_type=...  49.9 us
    all_gather x1, waiting for transfers between devices, body(): backward_key_piece = lax.all_gather(keys, 'ctx', axis=1, tiled=True)  46.5 us
    all_gather x1, waiting for transfers between devices, body(): backward_value_piece = lax.all_gather(values, 'ctx', axis=1, tiled=True)  43.5 us
    reduce_scatter x1, waiting for transfers between devices, body(): lax.psum_scatter(key_grad_all.astype(jnp.bfloat16), 'ctx', scatter_dimens...  43.1 us
  transfers between devices with their start and end apart: 23, of which 20 were waited for; matrix products, arithmetic and copies ran while one was open for 7% of the time, Pallas kernels for 0%

profile of v1, /device:TPU:0, one launch (start us, length us, event | category | flops | bytes accessed | tf_op | source)
XLA Modules:
  0.0 1076.3 jit_solution(5188700071178978599)
XLA Ops:
  8.8 10.2 all_gather.61
  19.0 8.3 all_gather.62
  27.3 7.5 all_gather.63
  35.2 2.3 fusion.96
  37.6 3.5 fusion.81
  41.3 2.4 fusion.78
  47.2 13.2 %all_gather.60 = s32[1,4096]{1,0:T(1,128)S(1)} all-gather(s32[1,1024]{1,0:T(1,128)S(1)} %copy-done.28), channel_id=1, replica_groups=mesh['dp'=2,'ctx'=4,'tp'=4] {'ctx'}, dimensions={1}, use_global_device_ids=true | all-gather | bytes 20480 | tf_op jit(solution)/shard_map/all_gather | solution.py:95
  64.4 7.0 all_gather.65
  71.4 57.5 %all-gather.16.cloned.1.call-done = bf16[2,4096,4,64]{1,3,2,0:T(8,128)(2,1)} async-done(((bf16[2,1024,4,64]{1,3,2,0:T(8,128)(2,1)}), bf16[2,4096,4,64]{1,3,2,0:T(8,128)(2,1)}) %all-gather.16.cloned.1.call-update) | async-done | bytes 4194320 | tf_op jit(solution)/shard_map/all_gather | solution.py:63
  128.9 83.7 %conditional.2 = (f32[1,4,1024]{2,1,0:T(4,128)S(1)}, f32[1,4,1024]{2,1,0:T(4,128)}, f32[1,1024,4,64]{1,3,2,0:T(8,128)S(1)}, f32[1,4,1024]{2,1,0:T(4,128)S(1)}) conditional(s32[]{:T(128)} %convert_element_type.302, () %tuple.32, (s32[1,1024]{1,0:T(1,128)S(1)}, s32[1,4096]{1,0:T(1,128)S(1)}, bf16[1,1024,4,64]{1,3,2,0:T(8,128)(2,1)S(1)}, ...), branch_computations={%region_4.0_spmd, %region_5.8_spmd} | conditional | flops 4483981312 | bytes 224088096 | solution.py:161
  129.1 4.7 broadcast_compare_fusion
  133.8 26.8 %fusion = (f32[4,1024]{1,0:T(4,128)S(1)}, f32[4,1024,4096]{2,1,0:T(8,128)}) fusion(pred[1024,4096]{1,0:T(8,128)(4,1)} %broadcast_compare_fusion, bf16[2,4096,4,64]{1,3,2,0:T(8,128)(2,1)} %get-tuple-element.53, bf16[1,1024,4,64]{1,3,2,0:T(8,128)(2,1)S(1)} %get-tuple-element.52), kind=kOutput, calls=%fused_computation.2 | convolution fusion | flops 2197811200 | bytes 73940992 | tf_op jit(solution)/shard_map/cond/branch_1_fun/sqhd,skhd->shqk/dot_general | solution.py:131
  160.6 23.3 %fusion.2 = f32[4,1024]{1,0:T(4,128)} fusion(f32[4,1024,4096]{2,1,0:T(8,128)} %get-tuple-element.155, f32[4,1024]{1,0:T(4,128)S(1)} %broadcast_maximum_fusion, pred[1024,4096]{1,0:T(8,128)(4,1)} %broadcast_compare_fusion), kind=kLoop, calls=%fused_computation.4 | loop fusion | flops 67104768 | bytes 71335936 | tf_op jit(solution)/shard_map/cond/branch_1_fun/reduce_sum | solution.py:151
  184.7 27.9 %fusion.16 = f32[1,1024,4,64]{1,3,2,0:T(8,128)S(1)} fusion(bf16[2,4096,4,64]{1,3,2,0:T(8,128)(2,1)} %get-tuple-element.53, f32[4,1024,4096]{2,1,0:T(8,128)} %get-tuple-element.155, f32[4,1024]{1,0:T(4,128)S(1)} %broadcast_maximum_fusion, pred[1024,4096]{1,0:T(8,128)(4,1)} %broadcast_compare_fusion, f32[1024,4]{0,1:T(4,128)S(1)} %get-tuple-element.144), kind=kOutput, calls=%fused_computation.14 | convolution fusion | flops 2214854656 | bytes 74481664 | tf_op jit(solution)/shard_map/cond/branch_1_fun/shqk,skhd->sqhd/dot_general | solution.py:152
  216.2 4.4 all-gather.1
  220.6 4.4 all-gather.2
  225.0 20.4 %reduce-scatter.13.cloned.1.call-done = bf16[256,1024]{1,0:T(8,128)(2,1)} async-done(((bf16[1024,1024]{1,0:T(8,128)(2,1)}), bf16[256,1024]{1,0:T(8,128)(2,1)}) %reduce-scatter.13.cloned.1.call-update) | async-done | bytes 524304 | tf_op jit(solution)/shard_map/reduce_scatter | solution.py:106
  248.3 2.3 fusion.115
  251.8 21.8 %all-gather.18.cloned.1.call-done = bf16[1024,1024]{1,0:T(8,128)(2,1)} async-done(((bf16[256,1024]{1,0:T(8,128)(2,1)}), bf16[1024,1024]{1,0:T(8,128)(2,1)}) %all-gather.18.cloned.1.call-update) | async-done | bytes 2097168 | tf_op jit(solution)/shard_map/all_gather | solution.py:111
  273.5 14.3 %fusion.52 = (bf16[1024,1024]{1,0:T(8,128)(2,1)}, f32[1024,1024]{1,0:T(8,128)}) fusion(bf16[1024,1024]{1,0:T(8,128)(2,1)} %all-gather.18.cloned.1.call-done, bf16[1024,1024]{1,0:T(8,128)(2,1)} %all-gather.20.cloned.1.call-done), kind=kOutput, calls=%fused_computation.48 | convolution fusion | flops 2215641088 | bytes 10485760 | tf_op jit(solution)/shard_map/dot_general | solution.py:169
  287.8 20.1 %all-gather.22.cloned.1.call-done = bf16[1024,1024]{1,0:T(8,128)(2,1)} async-done(((bf16[1024,512]{1,0:T(8,128)(2,1)}), bf16[1024,1024]{1,0:T(8,128)(2,1)}) %all-gather.22.cloned.1.call-update) | async-done | bytes 2097168 | tf_op jit(solution)/shard_map/all_gather | solution.py:87
  307.9 5.9 convolution_convert_fusion.3
  314.0 4.4 all-gather.3
  318.4 4.4 all-gather.4
  322.7 22.5 %reduce-scatter.15.cloned.1.call-done = bf16[256,1024]{1,0:T(8,128)(2,1)} async-done(((bf16[1024,1024]{1,0:T(8,128)(2,1)}), bf16[256,1024]{1,0:T(8,128)(2,1)}) %reduce-scatter.15.cloned.1.call-update) | async-done | bytes 524304 | tf_op jit(solution)/shard_map/reduce_scatter | solution.py:106
  349.3 2.5 fusion.122
  351.8 22.7 %all-gather.26.cloned.1.call-done = bf16[1024,1024]{1,0:T(8,128)(2,1)} async-done(((bf16[256,1024]{1,0:T(8,128)(2,1)}), bf16[1024,1024]{1,0:T(8,128)(2,1)}) %all-gather.26.cloned.1.call-update) | async-done | bytes 2097168 | tf_op jit(solution)/shard_map/all_gather | solution.py:111
  374.5 6.3 fusion.58
  382.2 3.7 convolution_convert_fusion.2
  386.2 31.1 %reduce-scatter.17.cloned.1.call-done = bf16[256,1024]{1,0:T(8,128)(2,1)} async-done(((bf16[1024,1024]{1,0:T(8,128)(2,1)}), bf16[256,1024]{1,0:T(8,128)(2,1)}) %reduce-scatter.17.cloned.1.call-update) | async-done | bytes 524304 | tf_op jit(solution)/shard_map/reduce_scatter | solution.py:106
  417.3 2.4 multiply_reduce_fusion
  419.7 2.8 fusion.121
  425.0 20.2 %all-gather.30.cloned.1.call-done = bf16[1024,1024]{1,0:T(8,128)(2,1)} async-done(((bf16[256,1024]{1,0:T(8,128)(2,1)}), bf16[1024,1024]{1,0:T(8,128)(2,1)}) %all-gather.30.cloned.1.call-update) | async-done | bytes 2097168 | tf_op jit(solution)/shard_map/all_gather | solution.py:111
  445.2 2.4 convolution_convert_fusion.6
  449.4 43.5 %all-gather.34.cloned.1.call-done = bf16[4096,4,64]{0,2,1:T(8,128)(2,1)} async-done(((bf16[1024,4,64]{0,2,1:T(8,128)(2,1)}), bf16[4096,4,64]{0,2,1:T(8,128)(2,1)}) %all-gather.34.cloned.1.call-update) | async-done | bytes 2097168 | tf_op jit(solution)/shard_map/all_gather | solution.py:205
  492.9 46.5 %all-gather.28.cloned.1.call-done = bf16[1,4096,4,64]{1,3,2,0:T(8,128)(2,1)} async-done(((bf16[1,1024,4,64]{1,3,2,0:T(8,128)(2,1)}), bf16[1,4096,4,64]{1,3,2,0:T(8,128)(2,1)}) %all-gather.28.cloned.1.call-update) | async-done | bytes 2097168 | tf_op jit(solution)/shard_map/all_gather | solution.py:204
  539.4 129.6 %conditional.3 = (bf16[1,4096,4,64]{1,3,2,0:T(8,128)(2,1)}, bf16[1,4096,4,64]{1,3,2,0:T(8,128)(2,1)}, f32[1,1024,4,32]{1,3,2,0:T(8,128)}, f32[1,1024,4,32]{1,3,2,0:T(8,128)S(1)}) conditional(s32[]{:T(128)} %convert_element_type.302, () %tuple.34, (s32[1,1024]{1,0:T(1,128)S(1)}, s32[1,4096]{1,0:T(1,128)S(1)}, ...), branch_computations={%region_20.21_spmd, %region_21.22_spmd} | conditional | flops 10911748096 | bytes 340906080 | solution.py:236
  539.4 4.7 broadcast_compare_fusion.1
  544.2 23.1 %fusion.36 = f32[4,1024,4096]{2,1,0:T(8,128)} fusion(bf16[1,4096,4,64]{1,3,2,0:T(8,128)(2,1)S(1)} %copy-done.1, bf16[1,1024,4,64]{1,3,2,0:T(8,128)(2,1)S(1)} %get-tuple-element.56), kind=kOutput, calls=%fused_computation.33 | convolution fusion | flops 2147483648 | bytes 69730304 | tf_op jit(solution)/shard_map/cond/branch_1_fun/sqhd,skhd->shqk/dot_general | solution.py:131
  567.3 28.2 %fusion.30 = bf16[1,4096,4,64]{1,3,2,0:T(8,128)(2,1)} fusion(f32[4,1024,4096]{2,1,0:T(8,128)} %fusion.36, f32[4,1024]{1,0:T(4,128)S(1)} %add_bitcast_fusion, pred[1024,4096]{1,0:T(8,128)(4,1)} %broadcast_compare_fusion.1, bf16[1,1024,4,64]{1,3,2,0:T(8,128)(2,1)S(1)} %copy-done.26), kind=kOutput, calls=%fused_computation.29 | convolution fusion | flops 2214592512 | bytes 73940992 | tf_op jit(solution)/shard_map/cond/branch_1_fun/shqk,sqhd->skhd/dot_general | solution.py:211
  595.6 41.7 %multiply_convert_fusion = bf16[4,1024,4096]{2,1,0:T(8,128)(2,1)} fusion(f32[4,1024,4096]{2,1,0:T(8,128)} %fusion.36, f32[4,1024]{1,0:T(4,128)S(1)} %bitcast.240, f32[4,1024]{1,0:T(4,128)S(1)} %add_bitcast_fusion, pred[1024,4096]{1,0:T(8,128)(4,1)} %broadcast_compare_fusion.1, bf16[1,4096,4,64]{1,3,2,0:T(8,128)(2,1)} %get-tuple-element.61, ...), kind=kOutput, calls=%fused_computation.21 | convolution fusion | flops 2248146944 | bytes 107511808 | tf_op jit(solution)/shard_map/cond/branch_1_fun/sqhd,skhd->shqk/dot_general | solution.py:217
  637.2 15.6 %fusion.41 = f32[1,1024,4,64]{1,3,2,0:T(8,128)S(1)} fusion(bf16[4,1024,4096]{2,1,0:T(8,128)(2,1)} %multiply_convert_fusion, bf16[1,4096,4,64]{1,3,2,0:T(8,128)(2,1)S(1)} %copy-done.1), kind=kOutput, calls=%fused_computation.36 | convolution fusion | flops 2147745792 | bytes 36700160 | tf_op jit(solution)/shard_map/cond/branch_1_fun/shqk,skhd->sqhd/dot_general | solution.py:222
  652.8 15.1 %fusion.29 = bf16[1,4096,4,64]{1,3,2,0:T(8,128)(2,1)} fusion(bf16[4,1024,4096]{2,1,0:T(8,128)(2,1)} %multiply_convert_fusion, bf16[1,1024,4,64]{1,3,2,0:T(8,128)(2,1)S(1)} %get-tuple-element.56), kind=kOutput, calls=%fused_computation.28 | convolution fusion | flops 2149580800 | bytes 36175872 | tf_op jit(solution)/shard_map/cond/branch_1_fun/shqk,sqhd->skhd/dot_general | solution.py:231
  670.8 5.3 convolution_convert_fusion.1
  676.2 6.0 convolution_convert_fusion
  682.3 3.3 convolution_convert_fusion.5
  685.6 26.0 %reduce-scatter.21.cloned.1.call-done = bf16[1,1024,4,64]{1,3,2,0:T(8,128)(2,1)} async-done(((bf16[1,4096,4,64]{1,3,2,0:T(8,128)(2,1)}), bf16[1,1024,4,64]{1,3,2,0:T(8,128)(2,1)}) %reduce-scatter.21.cloned.1.call-update) | async-done | bytes 524304 | tf_op jit(solution)/shard_map/reduce_scatter | solution.py:243
  711.6 2.5 fusion.102
  714.2 43.1 %reduce-scatter.19.cloned.1.call-done = bf16[1,1024,4,64]{1,3,2,0:T(8,128)(2,1)} async-done(((bf16[1,4096,4,64]{1,3,2,0:T(8,128)(2,1)}), bf16[1,1024,4,64]{1,3,2,0:T(8,128)(2,1)}) %reduce-scatter.19.cloned.1.call-update) | async-done | bytes 524304 | tf_op jit(solution)/shard_map/reduce_scatter | solution.py:240
  758.5 2.1 multiply_subtract_fusion
  771.4 19.9 %reduce-scatter.33.cloned.1.call-done = bf16[512,1024]{1,0:T(8,128)(2,1)} async-done(((bf16[1024,1024]{1,0:T(8,128)(2,1)}), bf16[512,1024]{1,0:T(8,128)(2,1)}) %reduce-scatter.33.cloned.1.call-update) | async-done | bytes 1048592 | tf_op jit(solution)/shard_map/reduce_scatter | solution.py:305
  791.3 34.0 %reduce-scatter.35.cloned.1.call-done = bf16[1024,512]{1,0:T(8,128)(2,1)} async-done(((bf16[1024,1024]{1,0:T(8,128)(2,1)}), bf16[1024,512]{1,0:T(8,128)(2,1)}) %reduce-scatter.35.cloned.1.call-update) | async-done | bytes 1048592 | tf_op jit(solution)/shard_map/reduce_scatter | solution.py:308
  825.3 16.9 %reduce-scatter.31.cloned.1.call-done = bf16[256,512]{1,0:T(8,128)(2,1)} async-done(((bf16[256,1024]{1,0:T(8,128)(2,1)}), bf16[256,512]{1,0:T(8,128)(2,1)}) %reduce-scatter.31.cloned.1.call-update) | async-done | bytes 262160 | tf_op jit(solution)/shard_map/reduce_scatter | solution.py:302
  842.2 17.3 %reduce-scatter.29.cloned.1.call-done = bf16[512,256]{0,1:T(8,128)(2,1)} async-done(((bf16[1024,256]{0,1:T(8,128)(2,1)}), bf16[512,256]{0,1:T(8,128)(2,1)}) %reduce-scatter.29.cloned.1.call-update) | async-done | bytes 262160 | tf_op jit(solution)/shard_map/reduce_scatter | solution.py:299
  859.6 17.5 %reduce-scatter.27.cloned.1.call-done = bf16[512,256]{0,1:T(8,128)(2,1)} async-done(((bf16[1024,256]{0,1:T(8,128)(2,1)}), bf16[512,256]{0,1:T(8,128)(2,1)}) %reduce-scatter.27.cloned.1.call-update) | async-done | bytes 262160 | tf_op jit(solution)/shard_map/reduce_scatter | solution.py:296
  877.1 17.3 %reduce-scatter.25.cloned.1.call-done = bf16[512,256]{0,1:T(8,128)(2,1)} async-done(((bf16[1024,256]{0,1:T(8,128)(2,1)}), bf16[512,256]{0,1:T(8,128)(2,1)}) %reduce-scatter.25.cloned.1.call-update) | async-done | bytes 262160 | tf_op jit(solution)/shard_map/reduce_scatter | solution.py:293
  894.5 34.1 %reduce-scatter.23.cloned.1.call-done = bf16[256,1024]{1,0:T(8,128)(2,1)} async-done(((bf16[1024,1024]{1,0:T(8,128)(2,1)}), bf16[256,1024]{1,0:T(8,128)(2,1)}) %reduce-scatter.23.cloned.1.call-update) | async-done | bytes 524304 | tf_op jit(solution)/shard_map/reduce_scatter | solution.py:106
  933.1 4.4 bitcast_convert_fusion.1
  937.5 5.3 all_gather.79
  942.9 5.0 all-reduce.6
  948.2 12.0 %all-reduce.4 = (bf16[512]{0:T(512)(128)(2,1)S(1)}, bf16[512]{0:T(512)(128)(2,1)S(1)}, bf16[512]{0:T(512)(128)(2,1)S(1)}, bf16[512]{0:T(512)(128)(2,1)S(1)}) all-reduce(bf16[512]{0:T(512)(128)(2,1)S(1)} %dynamic-slice.3, bf16[512]{0:T(512)(128)(2,1)S(1)} %dynamic-slice.5, ...), channel_id=1, replica_groups=mesh['dp'=2,'ctx'=4,'tp'=4] {'ctx'}, use_global_device_ids=true, to_apply=%region_43.44 | all-reduce | flops 2048 | bytes 8192 | tf_op jit(solution)/shard_map/psum | solution.py:331
  962.6 90.2 %all-reduce.9.cloned.1.call-done = (bf16[512,256]{0,1:T(8,128)(2,1)}, bf16[512,256]{0,1:T(8,128)(2,1)}, bf16[512,256]{0,1:T(8,128)(2,1)}, bf16[256,512]{1,0:T(8,...) async-done(((bf16[512,256]{0,1:T(8,128)(2,1)}, bf16[512,256]{0,1:T(8,128)(2,1)}, bf16[512,256]{0,1:T(8,128)(2,1)}, bf16[256,512]{1,0:T(8,128)(2,1)}, ...) | async-done | bytes 3145744 | tf_op jit(solution)/shard_map/psum | solution.py:325
  1060.3 2.8 convert_element_type.349
  1064.7 4.1 bitcast_convert_fusion
  (200 shorter events, 54.8 us)
Async XLA Ops:
  8.0 120.9 %all-gather.16.cloned.1.call-start = ((), (), s32[]{:S(2)}) async-start(), calls=%async_computation.12 | async-start | bytes 5242880 | tf_op jit(solution)/shard_map/all_gather | solution.py:63
  19.0 22.1 %copy-start.6 = (bf16[1024,256]{1,0:T(8,128)(2,1)}, bf16[1024,256]{1,0:T(8,128)(2,1)S(1)}, u32[]{:S(2)}) copy-start(bf16[1024,256]{1,0:T(8,128)(2,1)S(1)} %all_gather.61) | copy-start | bytes 1572868
  27.3 13.8 %copy-start.4 = (bf16[1024,256]{1,0:T(8,128)(2,1)}, bf16[1024,256]{1,0:T(8,128)(2,1)S(1)}, u32[]{:S(2)}) copy-start(bf16[1024,256]{1,0:T(8,128)(2,1)S(1)} %all_gather.62) | copy-start | bytes 1572868
  34.8 6.3 copy-start.2
  37.6 7.7 copy-start.16
  41.1 3.9 copy-start.23
  43.7 3.4 copy-start.28
  43.7 20.6 %copy-start.27 = (bf16[256,512]{1,0:T(8,128)(2,1)S(1)}, bf16[256,512]{1,0:T(8,128)(2,1)}, u32[]{:S(2)}) copy-start(bf16[256,512]{1,0:T(8,128)(2,1)} %param.24) | copy-start | bytes 786436
  45.0 19.3 %copy-start.20 = (f32[1024,32]{0,1:T(8,128)}, f32[1024,32]{0,1:T(8,128)S(1)}, u32[]{:S(2)}) copy-start(f32[1024,32]{0,1:T(8,128)S(1)} %get-tuple-element.171) | copy-start | bytes 393220
  45.3 0.7 copy-start.10
  47.1 198.3 %reduce-scatter.13.cloned.1.call-start = ((), (), s32[]{:S(2)}) async-start(), calls=%async_computation.13 | async-start | bytes 2621440 | tf_op jit(solution)/shard_map/reduce_scatter | solution.py:106
  71.4 142.0 %copy-start.17 = (bf16[256,1024]{1,0:T(8,128)(2,1)}, bf16[256,1024]{1,0:T(8,128)(2,1)S(1)}, u32[]{:S(2)}) copy-start(bf16[256,1024]{1,0:T(8,128)(2,1)S(1)} %all_gather.65) | copy-start | bytes 1572868
  212.6 3.6 copy-start.32
  212.6 8.0 copy-start.33
  213.5 34.9 %copy-start.14 = (bf16[1,1024,4,64]{1,3,2,0:T(8,128)(2,1)}, bf16[1,1024,4,64]{1,3,2,0:T(8,128)(2,1)S(1)}, u32[]{:S(2)}) copy-start(bf16[1,1024,4,64]{1,3,2,0:T(8,128)(2,1)S(1)} %fusion.116) | copy-start | bytes 1572868
  215.6 36.2 %all-gather.20.cloned.1.call-start = ((), (), s32[]{:S(2)}) async-start(), calls=%async_computation.15 | async-start | bytes 3145728 | tf_op jit(solution)/shard_map/all_gather | solution.py:86
  216.1 57.4 %all-gather.18.cloned.1.call-start = ((), (), s32[]{:S(2)}) async-start(), calls=%async_computation.14 | async-start | bytes 2621440 | tf_op jit(solution)/shard_map/all_gather | solution.py:111
  250.6 57.3 %all-gather.22.cloned.1.call-start = ((), (), s32[]{:S(2)}) async-start(), calls=%async_computation.16 | async-start | bytes 3145728 | tf_op jit(solution)/shard_map/all_gather | solution.py:87
  251.2 94.0 %reduce-scatter.15.cloned.1.call-start = ((), (), s32[]{:S(2)}) async-start(), calls=%async_computation.17 | async-start | bytes 2621440 | tf_op jit(solution)/shard_map/reduce_scatter | solution.py:106
  307.9 6.0 copy-start.34
  307.9 10.4 copy-start.35
  307.9 37.3 %copy-start = (bf16[256,1024]{1,0:T(8,128)(2,1)S(1)}, bf16[256,1024]{1,0:T(8,128)(2,1)}, u32[]{:S(2)}) copy-start(bf16[256,1024]{1,0:T(8,128)(2,1)} %reduce-scatter.13.cloned.1.call-done) | copy-start | bytes 1572868
  313.9 60.6 %all-gather.26.cloned.1.call-start = ((), (), s32[]{:S(2)}) async-start(), calls=%async_computation.19 | async-start | bytes 2621440 | tf_op jit(solution)/shard_map/all_gather | solution.py:111
  351.8 65.5 %reduce-scatter.17.cloned.1.call-start = ((), (), s32[]{:S(2)}) async-start(), calls=%async_computation.20 | async-start | bytes 2621440 | tf_op jit(solution)/shard_map/reduce_scatter | solution.py:106
  374.5 7.7 copy-start.37
  380.8 1.4 copy-start.39
  386.0 59.3 %all-gather.30.cloned.1.call-start = ((), (), s32[]{:S(2)}) async-start(), calls=%async_computation.22 | async-start | bytes 2621440 | tf_op jit(solution)/shard_map/all_gather | solution.py:111
  422.5 70.4 %all-gather.34.cloned.1.call-start = ((), (), s32[]{:S(2)}) async-start(), calls=%async_computation.33 | async-start | bytes 2621440 | tf_op jit(solution)/shard_map/all_gather | solution.py:205
  423.1 116.3 %all-gather.28.cloned.1.call-start = ((), (), s32[]{:S(2)}) async-start(), calls=%async_computation.21 | async-start | bytes 2621440 | tf_op jit(solution)/shard_map/all_gather | solution.py:204
  425.0 286.6 %reduce-scatter.21.cloned.1.call-start = ((), (), s32[]{:S(2)}) async-start(), calls=%async_computation.24 | async-start | bytes 2621440 | tf_op jit(solution)/shard_map/reduce_scatter | solution.py:243
  447.7 0.8 copy-start.25
  539.4 4.8 copy-start.1
  544.2 23.1 %copy-start.26 = (bf16[1,1024,4,64]{1,3,2,0:T(8,128)(2,1)S(1)}, bf16[1,1024,4,64]{1,3,2,0:T(8,128)(2,1)}, u32[]{:S(2)}) copy-start(bf16[1,1024,4,64]{1,3,2,0:T(8,128)(2,1)} %get-tuple-element.60) | copy-start | bytes 1572868 | tf_op jit(solution)/shard_map/cond
  669.0 7.1 copy-start.18
  669.0 1.8 copy-start.36
  669.0 88.3 %reduce-scatter.19.cloned.1.call-start = ((), (), s32[]{:S(2)}) async-start(), calls=%async_computation.23 | async-start | bytes 2621440 | tf_op jit(solution)/shard_map/reduce_scatter | solution.py:240
  669.8 121.5 %reduce-scatter.33.cloned.1.call-start = ((), (), s32[]{:S(2)}) async-start(), calls=%async_computation.31 | async-start | bytes 3145728 | tf_op jit(solution)/shard_map/reduce_scatter | solution.py:305
  676.1 6.1 copy-start.15
  676.1 149.2 %reduce-scatter.35.cloned.1.call-start = ((), (), s32[]{:S(2)}) async-start(), calls=%async_computation.32 | async-start | bytes 3145728 | tf_op jit(solution)/shard_map/reduce_scatter | solution.py:308
  682.2 29.5 %copy-start.8 = (bf16[1,1024,1024]{2,1,0:T(8,128)(2,1)S(1)}, bf16[1,1024,1024]{2,1,0:T(8,128)(2,1)}, u32[]{:S(2)}) copy-start(bf16[1,1024,1024]{2,1,0:T(8,128)(2,1)} %param.18) | copy-start | bytes 6291460
  682.2 76.3 %copy-start.19 = (f32[1,1024,4,32]{1,3,2,0:T(8,128)S(1)}, f32[1,1024,4,32]{1,3,2,0:T(8,128)}, u32[]{:S(2)}) copy-start(f32[1,1024,4,32]{1,3,2,0:T(8,128)} %copy-done.18) | copy-start | bytes 1572868
  682.2 76.3 %copy-start.21 = (f32[1024,32]{0,1:T(8,128)S(1)}, f32[1024,32]{0,1:T(8,128)}, u32[]{:S(2)}) copy-start(f32[1024,32]{0,1:T(8,128)} %copy-done.20) | copy-start | bytes 393220
  682.2 160.0 %reduce-scatter.31.cloned.1.call-start = ((), (), s32[]{:S(2)}) async-start(), calls=%async_computation.30 | async-start | bytes 786432 | tf_op jit(solution)/shard_map/reduce_scatter | solution.py:302
  685.6 174.0 %reduce-scatter.29.cloned.1.call-start = ((), (), s32[]{:S(2)}) async-start(), calls=%async_computation.29 | async-start | bytes 786432 | tf_op jit(solution)/shard_map/reduce_scatter | solution.py:299
  714.2 162.9 %reduce-scatter.27.cloned.1.call-start = ((), (), s32[]{:S(2)}) async-start(), calls=%async_computation.28 | async-start | bytes 786432 | tf_op jit(solution)/shard_map/reduce_scatter | solution.py:296
  760.7 2.6 copy-start.11
  760.7 5.0 copy-start.7
  762.2 132.2 %reduce-scatter.25.cloned.1.call-start = ((), (), s32[]{:S(2)}) async-start(), calls=%async_computation.27 | async-start | bytes 786432 | tf_op jit(solution)/shard_map/reduce_scatter | solution.py:293
  763.3 0.8 copy-start.13
  764.1 3.6 copy-start.5
  765.6 2.1 copy-start.12
  765.6 2.8 copy-start.3
  765.6 2.8 copy-start.24
  765.6 162.9 %reduce-scatter.23.cloned.1.call-start = ((), (), s32[]{:S(2)}) async-start(), calls=%async_computation.25 | async-start | bytes 2621440 | tf_op jit(solution)/shard_map/reduce_scatter | solution.py:106
  770.6 158.0 %copy-start.9 = (f32[256,1024]{1,0:T(8,128)S(1)}, f32[256,1024]{1,0:T(8,128)}, u32[]{:S(2)}) copy-start(f32[256,1024]{1,0:T(8,128)} %get-tuple-element.147) | copy-start | bytes 3145732
  770.6 161.2 %copy-start.38 = (u32[32]{0:T(128)S(1)}, u32[32]{0:T(128)}, u32[]{:S(2)}) copy-start(u32[32]{0:T(128)} %constant.140) | copy-start | bytes 388
  770.6 162.4 %copy-start.29 = (bf16[1024]{0:T(1024)(128)(2,1)S(1)}, bf16[1024]{0:T(1024)(128)(2,1)}, u32[]{:S(2)}) copy-start(bf16[1024]{0:T(1024)(128)(2,1)} %get-tuple-element.117) | copy-start | bytes 6148
  770.6 162.5 %all-gather.24.cloned.1.call-start = ((), (), s32[]{:S(2)}) async-start(), calls=%async_computation.18 | async-start | bytes 2621440 | tf_op jit(solution)/shard_map/all_gather | solution.py:277
  771.3 281.5 %all-reduce.9.cloned.1.call-start = ((), (), s32[]{:S(2)}) async-start(), calls=%async_computation.34 | async-start | bytes 6291456 | tf_op jit(solution)/shard_map/psum | solution.py:325
  894.5 170.3 %all-gather.32.cloned.1.call-start = ((), (), s32[]{:S(2)}) async-start(), calls=%async_computation.26 | async-start | bytes 2621440 | tf_op jit(solution)/shard_map/all_gather | solution.py:278
  930.6 6.9 copy-start.31
  930.6 6.9 copy-start.30
  1052.8 10.3 copy-start.22
Sparse Core Ops, SparseCore 0:
  47.2 81.6 all-gather.15
  215.7 29.6 reduce-scatter.12
  351.9 22.5 all-gather.25
  422.6 22.5 all-gather.29
  447.2 45.6 all-gather.33
  494.9 44.4 all-gather.27
  669.2 42.4 reduce-scatter.20
  714.5 42.8 reduce-scatter.18
  760.2 31.0 reduce-scatter.32
  793.4 31.8 reduce-scatter.34
  827.6 14.6 reduce-scatter.30
  844.9 14.6 reduce-scatter.28
  862.4 14.6 reduce-scatter.26
  879.8 14.6 reduce-scatter.24
  897.4 31.1 reduce-scatter.22
  931.3 121.4 all-reduce.8
Sparse Core Ops, SparseCore 1:
  217.6 31.4 all-gather.19
  251.1 22.4 all-gather.17
  274.9 32.9 all-gather.21
  314.0 31.2 reduce-scatter.14
  386.0 31.2 reduce-scatter.16
  773.5 21.8 all-gather.23
  930.7 22.5 all-gather.31
